TPU v7x, 32 devices: a whole 2x2x4 slice. The times are simulated.
32 devices in a mesh: band: 4 (over y, x), domain: 8 (over z, core).
Axes of the slice: x: 2, y: 2, z: 4, core: 2. Of those that a mesh axis runs over, the one named last changes fastest.
Arguments:
- orbitals: float32 [6144, 512], P('domain', 'band'), may hold values from -6 to 6
- potential: float32 [6144], P('domain'), may hold values from -1 to 1
- occupation: float32 [512], P('band'), may hold values from 0 to 0.0068359375, as said below
- cell_matrix: bfloat16 [343, 343], replicated, may hold values from -1 to 2, as said below
- cell_nodes: int32 [32, 343], P('domain'), may hold values from 0 to 936, as said below
- face_order: int32 [8, 169], P('domain'), may hold values from 0 to 168, as said below
- pois_matrix: float32 [729, 729], replicated, may hold values from -1 to 2, as said below
- pois_nodes: int32 [16, 729], P('domain'), may hold values from 0 to 848, as said below
- pois_face: int32 [8, 81], P('domain'), may hold values from 0 to 80, as said below
- screening: float32 [6144], P('domain'), may hold values from 0.5 to 2
- block_owner: int32 [8, 8], P('domain'), may hold values from 0 to 7, as said below
Outputs:
- filtered: float32 [6144, 512], P('domain', 'band')
- hartree: float32 [6144], P('domain')
Inputs may be any that keep to these rules, and one draw needn't show every extreme that they name: `occupation`: positive weights. `cell_matrix`: symmetric. `pois_matrix`: symmetric. `cell_nodes`: cell c (counted from 0 within its domain) uses the local nodes (c * 234 + k) mod 937 for k < 343, in a drawn order. `pois_nodes`: cell c (counted from 0 within its domain) uses the local nodes (c * 424 + k) mod 849 for k < 729, in a drawn order. `face_order`: each row is a permutation. `pois_face`: each row is a permutation. `block_owner`: each row is a permutation.
All inputs are finite; a program needn't handle non-finite values.
Results may differ from a plain program's by a relative error of at most 0.0065.
The roundings to bfloat16 on the way count: a program that leaves them out, or rounds other values in their place, can miss the bound.
Values may be sent and summed in bfloat16 or wider, within the bound.
No kernel may reach another device: no remote copies, remote signals or barrier semaphores. Data moves between devices by JAX's collectives and lax.ppermute only.
A program may use at most 64 MiB of HBM per device.

v0:
```python
import jax
import jax.numpy as jnp
from jax import lax
from jax.sharding import PartitionSpec as P

filter_center = 1.8
filter_half = 2.7
solve_center = 3.25
solve_half = 2.75
solve_ratio = solve_center / solve_half
weight_zero = 1.0 / solve_ratio
weight_one = 1.0 / (2.0 * solve_ratio - weight_zero)
weight_two = 1.0 / (2.0 * solve_ratio - weight_one)


def from_behind(array, axis, by):
    length = lax.axis_size(axis)
    return lax.ppermute(array, axis, [(i, (i + by) % length) for i in range(length)])


def filter_step(applied, current, earlier):
    if earlier is None:
        return (applied - filter_center * current) / filter_half
    return 2.0 * (applied - filter_center * current) / filter_half - earlier


def next_rows(values, face_row):
    coming = from_behind(values, "domain", -1)
    return jnp.take(coming, face_row, axis=0)


def next_low_rows(values, face_row):
    coming = from_behind(values, "domain", -1)
    return jnp.take(coming, face_row, axis=0)


def fold_back(upper_rows, face_row):
    ordered = jnp.zeros_like(upper_rows).at[face_row].set(upper_rows)
    return from_behind(ordered, "domain", 1)


def assembled(owned_rows, face_row, terms):
    owned_count = owned_rows.shape[0]
    shared = face_row.shape[0]
    local_rows = jnp.concatenate([owned_rows, next_rows(owned_rows[:shared], face_row)], axis=0)
    partial_value = terms(local_rows)
    arrived = fold_back(partial_value[owned_count:], face_row)
    return partial_value[:owned_count].at[:shared].add(arrived)


def assembled_low(owned_rows, face_row, terms):
    owned_count = owned_rows.shape[0]
    shared = face_row.shape[0]
    low_rows = owned_rows.astype(jnp.bfloat16)
    local_rows = jnp.concatenate([low_rows, next_low_rows(low_rows[:shared], face_row)], axis=0)
    partial_value = terms(local_rows)
    arrived = fold_back(partial_value[owned_count:], face_row)
    return partial_value[:owned_count].at[:shared].add(arrived)


def cell_terms(local_rows, cell_matrix, node_ids):
    cell_vals = jnp.take(local_rows, node_ids, axis=0)
    product = jnp.einsum("pq,cqm->cpm", cell_matrix, cell_vals, preferred_element_type=jnp.float32)
    columns = local_rows.shape[1]
    return (
        jnp.zeros(local_rows.shape, jnp.float32)
        .at[node_ids.reshape(-1)]
        .add(product.reshape(-1, columns))
    )


def field_terms(local_rows, pois_matrix, node_ids):
    cell_vals = jnp.take(local_rows, node_ids, axis=0)
    product = jnp.einsum(
        "pq,cq->cp",
        pois_matrix,
        cell_vals,
        precision=lax.Precision.HIGHEST,
        preferred_element_type=jnp.float32,
    )
    return (
        jnp.zeros(local_rows.shape, jnp.float32).at[node_ids.reshape(-1)].add(product.reshape(-1))
    )


def reshuffle(blocks):
    return lax.all_to_all(blocks, "domain", split_axis=0, concat_axis=0, tiled=True)


def band_total(values):
    return lax.psum(values, "band")


def per_device(
    orbitals,
    potential,
    occupation,
    cell_matrix,
    cell_nodes,
    face_order,
    pois_matrix,
    pois_nodes,
    pois_face,
    screening,
    block_owner,
):
    domains = lax.axis_size("domain")
    owned_count = orbitals.shape[0]
    block_len = owned_count // domains
    face_row = face_order[0]
    owner_row = block_owner[0]
    field_face = pois_face[0]

    def orbital_terms(local_rows):
        return cell_terms(local_rows, cell_matrix, cell_nodes)

    def hamiltonian(vector, potential_in):
        return assembled_low(vector, face_row, orbital_terms) + potential_in[:, None] * vector

    filter_one = filter_step(hamiltonian(orbitals, potential), orbitals, None)
    filter_two = filter_step(hamiltonian(filter_one, potential), filter_one, orbitals)
    filter_three = filter_step(hamiltonian(filter_two, potential), filter_two, filter_one)
    partial_value = jnp.dot(
        filter_three * filter_three,
        occupation,
        precision=lax.Precision.HIGHEST,
        preferred_element_type=jnp.float32,
    )
    summed = band_total(partial_value)
    arranged = (
        jnp.zeros((domains, block_len), jnp.float32)
        .at[owner_row]
        .set(summed.reshape(domains, block_len))
    )
    source = reshuffle(arranged).reshape(owned_count)

    def field_operator(vector):
        return (
            assembled(
                vector,
                field_face,
                lambda local_rows: field_terms(local_rows, pois_matrix, pois_nodes),
            )
            + screening * vector
        )

    step_one = source / solve_center
    residual = source - field_operator(step_one)
    step_two = weight_one * weight_zero * step_one + 2.0 * weight_one / solve_half * residual
    residual = residual - field_operator(step_two)
    step_three = weight_two * weight_one * step_two + 2.0 * weight_two / solve_half * residual
    solution = step_one + step_two + step_three
    returned = reshuffle(solution.reshape(domains, block_len))
    hartree = jnp.take(returned, owner_row, axis=0).reshape(owned_count)
    potential_new = potential + hartree
    refilter_one = filter_step(hamiltonian(filter_three, potential_new), filter_three, None)
    refilter_two = filter_step(hamiltonian(refilter_one, potential_new), refilter_one, filter_three)
    return (refilter_two, hartree)


def solution(mesh):
    return jax.shard_map(
        per_device,
        mesh=mesh,
        in_specs=(
            P("domain", "band"),
            P("domain"),
            P("band"),
            P(),
            P("domain", None),
            P("domain", None),
            P(),
            P("domain", None),
            P("domain", None),
            P("domain"),
            P("domain", None),
        ),
        out_specs=(P("domain", "band"), P("domain")),
        check_vma=False,
    )
```

profile of v0, /device:TPU:0, one launch (start us, length us, event | category | flops | bytes accessed | tf_op | source)
XLA Modules:
  0.0 261.4 jit_solution(17496827061707327766)
XLA Ops:
  1.8 4.6 %collective-permute-start = (bf16[169,128]{1,0:T(8,128)(2,1)S(1)}, bf16[169,128]{1,0:T(8,128)(2,1)S(1)}, u32[]{:S(2)}, u32[]{:S(2)}) collective-permute-start(bf16[169,128]{1,0:T(8,128)(2,1)S(1)} %slice.251), channel_id=1, source_target_pairs={{0,7},{1,0},{2,1},{3,2},{4,3},{5,4},{6,5},{7,6},{8,15},{9,8},{10,9... | collective-permute-start | bytes 129800 | tf_op jit(solution)/shard_map/ppermute | solution.py:18
  13.0 3.3 %gather_fusion.2 = bf16[1372,128]{1,0:T(8,128)(2,1)S(1)} fusion(bf16[937,128]{1,0:T(8,128)(2,1)S(1)} %pad_maximum_fusion, s32[2048]{0:T(1024)S(1)} %pad_clamp_fusion.1), kind=kCustom, calls=%fused_computation.1.clone | custom fusion | bytes 707952 | tf_op jit(solution)/shard_map/jit(_take)/gather | solution.py:62
  19.9 9.9 %scatter_custom_fusion = f32[937,128]{1,0:T(8,128)} fusion(s32[1372]{0:T(1024)S(1)} %fusion.51, f32[1372,128]{1,0:T(8,128)} %reshape.513, f32[]{:T(128)} %constant.233.clone.1), kind=kCustom, calls=%fused_computation.72 | custom fusion | flops 175616 | bytes 480256 | tf_op jit(solution)/shard_map/scatter-add | solution.py:68
  32.8 4.1 %collective-permute-done.1 = f32[169,128]{1,0:T(8,128)S(1)} collective-permute-done((f32[169,128]{1,0:T(8,128)S(1)}, f32[169,128]{1,0:T(8,128)S(1)}, u32[]{:S(2)}, u32[]{:S(2)}) %collective-permute-start.1) | collective-permute-done | bytes 86560 | tf_op jit(solution)/shard_map/ppermute | solution.py:18
  43.7 4.4 %gather_fusion.4 = bf16[1372,128]{1,0:T(8,128)(2,1)} fusion(bf16[937,128]{1,0:T(8,128)(2,1)S(1)} %pad_maximum_fusion.1, s32[2048]{0:T(1024)} %copy-done.7), kind=kCustom, calls=%fused_computation.8.clone | custom fusion | bytes 707952 | tf_op jit(solution)/shard_map/jit(_take)/gather | solution.py:62
  49.9 2.4 convolution_bitcast_fusion.3
  52.4 2.1 reshape.529
  54.4 9.9 %scatter_custom_fusion.2 = f32[937,128]{1,0:T(8,128)} fusion(s32[1372]{0:T(1024)} %copy-done.25, f32[1372,128]{1,0:T(8,128)} %reshape.529, f32[]{:T(128)} %constant.233.clone.1), kind=kCustom, calls=%fused_computation.70 | custom fusion | flops 175616 | bytes 480256 | tf_op jit(solution)/shard_map/scatter-add | solution.py:68
  68.1 3.4 %collective-permute-done.3 = f32[169,128]{1,0:T(8,128)S(1)} collective-permute-done((f32[169,128]{1,0:T(8,128)S(1)}, f32[169,128]{1,0:T(8,128)S(1)}, u32[]{:S(2)}, u32[]{:S(2)}) %collective-permute-start.3) | collective-permute-done | bytes 86560 | tf_op jit(solution)/shard_map/ppermute | solution.py:18
  79.1 4.0 %gather_fusion.6 = bf16[1372,128]{1,0:T(8,128)(2,1)} fusion(bf16[937,128]{1,0:T(8,128)(2,1)S(1)} %pad_maximum_fusion.2, s32[2048]{0:T(1024)S(1)} %copy-done.8), kind=kCustom, calls=%fused_computation.9.clone | custom fusion | bytes 707952 | tf_op jit(solution)/shard_map/jit(_take)/gather | solution.py:62
  87.6 9.9 %scatter_custom_fusion.4 = f32[937,128]{1,0:T(8,128)} fusion(s32[1372]{0:T(1024)} %copy-done.25, f32[1372,128]{1,0:T(8,128)} %reshape.545, f32[]{:T(128)} %constant.233.clone.1), kind=kCustom, calls=%fused_computation.68 | custom fusion | flops 175616 | bytes 480256 | tf_op jit(solution)/shard_map/scatter-add | solution.py:68
  100.7 4.0 %collective-permute-done.5 = f32[169,128]{1,0:T(8,128)S(1)} collective-permute-done((f32[169,128]{1,0:T(8,128)S(1)}, f32[169,128]{1,0:T(8,128)S(1)}, u32[]{:S(2)}, u32[]{:S(2)}) %collective-permute-start.5) | collective-permute-done | bytes 86560 | tf_op jit(solution)/shard_map/ppermute | solution.py:18
  109.9 9.9 %psum.7 = f32[8,96]{1,0:T(8,128)S(1)} all-reduce(f32[8,96]{1,0:T(8,128)S(1)} %reshape.383), channel_id=1, replica_groups=mesh['band'=4,'domain'=8] {'band'}, use_global_device_ids=true, to_apply=%region_8.11 | all-reduce | flops 768 | bytes 6144 | tf_op jit(solution)/shard_map/psum | solution.py:91
  121.1 3.3 %all-to-all-start = ((f32[8,1,96]{2,1,0:T(1,128)}), f32[8,1,96]{2,1,0:T(1,128)S(1)}, u32[]{:S(2)}, u32[]{:S(2)}) async-start(f32[8,1,96]{2,1,0:T(1,128)} %bitcast.12), calls=%async_computation | async-start | bytes 8192 | tf_op jit(solution)/shard_map/all_to_all | solution.py:87
  124.4 5.4 %all-to-all-done = f32[8,1,96]{2,1,0:T(1,128)S(1)} async-done(((f32[8,1,96]{2,1,0:T(1,128)}), f32[8,1,96]{2,1,0:T(1,128)S(1)}, u32[]{:S(2)}, u32[]{:S(2)}) %all-to-all-start) | async-done | bytes 3104 | tf_op jit(solution)/shard_map/all_to_all | solution.py:87
  134.3 5.6 %gather_fusion.10 = f32[1458]{0:T(1024)S(1)} fusion(f32[849]{0:T(1024)S(1)} %pad_maximum_fusion.5, s32[2048]{0:T(1024)S(1)} %pad_clamp_fusion), kind=kCustom, calls=%fused_computation.3.clone | custom fusion | bytes 17496 | tf_op jit(solution)/shard_map/jit(_take)/gather | solution.py:73
  142.2 11.0 %scatter_custom_fusion.9 = f32[849]{0:T(1024)S(1)} fusion(s32[1458]{0:T(1024)S(1)} %fusion.46, f32[1458]{0:T(1024)S(1)} %reshape.585, f32[]{:T(128)} %constant.233.clone.1), kind=kCustom, calls=%fused_computation.137 | custom fusion | flops 1458 | bytes 3400 | tf_op jit(solution)/shard_map/scatter-add | solution.py:82
  155.7 3.3 %collective-permute-done.9 = f32[81]{0:T(128)S(1)} collective-permute-done((f32[81]{0:T(128)S(1)}, f32[81]{0:T(128)S(1)}, u32[]{:S(2)}, u32[]{:S(2)}) %collective-permute-start.9) | collective-permute-done | bytes 356 | tf_op jit(solution)/shard_map/ppermute | solution.py:18
  161.9 5.7 %gather_fusion.12 = f32[1458]{0:T(1024)S(1)} fusion(f32[849]{0:T(1024)S(1)} %pad_maximum_fusion.6, s32[2048]{0:T(1024)S(1)} %pad_clamp_fusion), kind=kCustom, calls=%fused_computation.13.clone | custom fusion | bytes 17496 | tf_op jit(solution)/shard_map/jit(_take)/gather | solution.py:73
  169.7 11.0 %scatter_custom_fusion.11 = f32[849]{0:T(1024)S(1)} fusion(s32[1458]{0:T(1024)S(1)} %fusion.46, f32[1458]{0:T(1024)S(1)} %reshape.601, f32[]{:T(128)} %constant.233.clone.1), kind=kCustom, calls=%fused_computation.135 | custom fusion | flops 1458 | bytes 3400 | tf_op jit(solution)/shard_map/scatter-add | solution.py:82
  181.8 4.7 %collective-permute-done.11 = f32[81]{0:T(128)S(1)} collective-permute-done((f32[81]{0:T(128)S(1)}, f32[81]{0:T(128)S(1)}, u32[]{:S(2)}, u32[]{:S(2)}) %collective-permute-start.11) | collective-permute-done | bytes 356 | tf_op jit(solution)/shard_map/ppermute | solution.py:18
  187.3 3.3 %all-to-all-start.1 = ((f32[8,1,96]{2,1,0:T(1,128)}), f32[8,1,96]{2,1,0:T(1,128)S(1)}, u32[]{:S(2)}, u32[]{:S(2)}) async-start(f32[8,1,96]{2,1,0:T(1,128)} %all_to_all.16), calls=%async_computation.1 | async-start | bytes 8192 | tf_op jit(solution)/shard_map/all_to_all | solution.py:87
  190.6 3.5 %collective-permute-start.6 = (bf16[169,128]{1,0:T(8,128)(2,1)S(1)}, bf16[169,128]{1,0:T(8,128)(2,1)S(1)}, u32[]{:S(2)}, u32[]{:S(2)}) collective-permute-start(bf16[169,128]{1,0:T(8,128)(2,1)S(1)} %slice.263), channel_id=1, source_target_pairs={{0,7},{1,0},{2,1},{3,2},{4,3},{5,4},{6,5},{7,6},{8,15},{9,8},{10,9... | collective-permute-start | bytes 129800 | tf_op jit(solution)/shard_map/ppermute | solution.py:18
  197.6 4.0 %gather_fusion.8 = bf16[1372,128]{1,0:T(8,128)(2,1)} fusion(bf16[937,128]{1,0:T(8,128)(2,1)S(1)} %pad_maximum_fusion.3, s32[2048]{0:T(1024)S(1)} %copy-done.8), kind=kCustom, calls=%fused_computation.10.clone | custom fusion | bytes 707952 | tf_op jit(solution)/shard_map/jit(_take)/gather | solution.py:62
  204.2 2.0 reshape.561
  206.2 9.3 %scatter_custom_fusion.6 = f32[937,128]{1,0:T(8,128)S(1)} fusion(s32[1372]{0:T(1024)} %copy-done.25, f32[1372,128]{1,0:T(8,128)} %reshape.561, f32[]{:T(128)} %constant.233.clone.1), kind=kCustom, calls=%fused_computation.66 | custom fusion | flops 175616 | bytes 480256 | tf_op jit(solution)/shard_map/scatter-add | solution.py:68
  218.8 4.3 %collective-permute-done.7 = f32[169,128]{1,0:T(8,128)S(1)} collective-permute-done((f32[169,128]{1,0:T(8,128)}, f32[169,128]{1,0:T(8,128)S(1)}, u32[]{:S(2)}, u32[]{:S(2)}) %collective-permute-start.7) | collective-permute-done | bytes 86560 | tf_op jit(solution)/shard_map/ppermute | solution.py:18
  229.2 4.4 %gather_fusion.14 = bf16[1372,128]{1,0:T(8,128)(2,1)} fusion(bf16[937,128]{1,0:T(8,128)(2,1)S(1)} %pad_maximum_fusion.4, s32[2048]{0:T(1024)} %copy-done.7), kind=kCustom, calls=%fused_computation.11.clone | custom fusion | bytes 707952 | tf_op jit(solution)/shard_map/jit(_take)/gather | solution.py:62
  235.4 2.4 convolution_bitcast_fusion
  239.7 9.9 %scatter_custom_fusion.13 = f32[937,128]{1,0:T(8,128)} fusion(s32[1372]{0:T(1024)} %copy-done.25, f32[1372,128]{1,0:T(8,128)} %reshape.617, f32[]{:T(128)} %constant.233.clone.1), kind=kCustom, calls=%fused_computation.64 | custom fusion | flops 175616 | bytes 480256 | tf_op jit(solution)/shard_map/scatter-add | solution.py:68
  252.8 4.0 %collective-permute-done.13 = f32[169,128]{1,0:T(8,128)S(1)} collective-permute-done((f32[169,128]{1,0:T(8,128)S(1)}, f32[169,128]{1,0:T(8,128)S(1)}, u32[]{:S(2)}, u32[]{:S(2)}) %collective-permute-start.13) | collective-permute-done | bytes 86560 | tf_op jit(solution)/shard_map/ppermute | solution.py:18
  259.4 2.0 multiply_subtract_fusion
  (198 shorter events, 88.9 us)
Async XLA Ops:
  0.6 139.5 %copy-start = (f32[729,729]{1,0:T(8,128)S(1)}, f32[729,729]{1,0:T(8,128)}, u32[]{:S(2)}) copy-start(f32[729,729]{1,0:T(8,128)} %param.39) | copy-start | bytes 6377296
  1.8 10.3 %collective-permute-start = (bf16[169,128]{1,0:T(8,128)(2,1)S(1)}, bf16[169,128]{1,0:T(8,128)(2,1)S(1)}, u32[]{:S(2)}, u32[]{:S(2)}) collective-permute-start(bf16[169,128]{1,0:T(8,128)(2,1)S(1)} %slice.251), channel_id=1, source_target_pairs={{0,7},{1,0},{2,1},{3,2},{4,3},{5,4},{6,5},{7,6},{8,15},{9,8},{10,9... | collective-permute-start | bytes 129800 | tf_op jit(solution)/shard_map/ppermute | solution.py:18
  16.5 22.1 %copy-start.2 = (f32[768,128]{1,0:T(8,128)S(1)}, f32[768,128]{1,0:T(8,128)}, u32[]{:S(2)}) copy-start(f32[768,128]{1,0:T(8,128)} %param.33) | copy-start | bytes 1179652
  31.1 5.8 %collective-permute-start.1 = (f32[169,128]{1,0:T(8,128)S(1)}, f32[169,128]{1,0:T(8,128)S(1)}, u32[]{:S(2)}, u32[]{:S(2)}) collective-permute-start(f32[169,128]{1,0:T(8,128)S(1)} %scatter_custom_fusion.1), channel_id=1, source_target_pairs={{0,1},{1,2},{2,3},{3,4},{4,5},{5,6},{6,7},{7,0},{8,9},{9,10},{10,1... | collective-permute-start | bytes 259592 | tf_op jit(solution)/shard_map/ppermute | solution.py:18
  39.5 1.8 collective-permute-start.2
  49.9 24.1 %copy-start.4 = (f32[768,128]{1,0:T(8,128)S(1)}, f32[768,128]{1,0:T(8,128)}, u32[]{:S(2)}) copy-start(f32[768,128]{1,0:T(8,128)} %copy-done.3) | copy-start | bytes 1179652
  49.9 24.1 %copy-start.10 = (f32[768]{0:T(1024)S(1)}, f32[768]{0:T(1024)}, u32[]{:S(2)}) copy-start(f32[768]{0:T(1024)} %param.34) | copy-start | bytes 9220
  49.9 24.1 %copy-start.14 = (f32[768]{0:T(1024)S(1)}, f32[768]{0:T(1024)}, u32[]{:S(2)}) copy-start(f32[768]{0:T(1024)} %broadcast_multiply_fusion.2) | copy-start | bytes 9220
  52.4 23.4 %copy-start.30 = (s32[1,8]{1,0:T(1,128)S(1)}, s32[1,8]{1,0:T(1,128)}, u32[]{:S(2)}) copy-start(s32[1,8]{1,0:T(1,128)} %param.43) | copy-start | bytes 100
  52.4 23.9 %copy-start.11 = (s32[2,729]{1,0:T(2,128)S(1)}, s32[2,729]{1,0:T(2,128)}, u32[]{:S(2)}) copy-start(s32[2,729]{1,0:T(2,128)} %param.40) | copy-start | bytes 17500
  52.4 24.0 %copy-start.17 = (s32[2,729]{1,0:T(2,128)S(1)}, s32[2,729]{1,0:T(2,128)}, u32[]{:S(2)}) copy-start(s32[2,729]{1,0:T(2,128)} %compare_select_fusion.2) | copy-start | bytes 17500
  54.4 24.6 %copy-start.8 = (s32[2048]{0:T(1024)S(1)}, s32[2048]{0:T(1024)}, u32[]{:S(2)}) copy-start(s32[2048]{0:T(1024)} %copy-done.7) | copy-start | bytes 24580
  65.7 5.8 %collective-permute-start.3 = (f32[169,128]{1,0:T(8,128)S(1)}, f32[169,128]{1,0:T(8,128)S(1)}, u32[]{:S(2)}, u32[]{:S(2)}) collective-permute-start(f32[169,128]{1,0:T(8,128)S(1)} %scatter_custom_fusion.3), channel_id=1, source_target_pairs={{0,1},{1,2},{2,3},{3,4},{4,5},{5,6},{6,7},{7,0},{8,9},{9,10},{10,1... | collective-permute-start | bytes 259592 | tf_op jit(solution)/shard_map/ppermute | solution.py:18
  75.3 2.1 collective-permute-start.4
  98.8 5.8 %collective-permute-start.5 = (f32[169,128]{1,0:T(8,128)S(1)}, f32[169,128]{1,0:T(8,128)S(1)}, u32[]{:S(2)}, u32[]{:S(2)}) collective-permute-start(f32[169,128]{1,0:T(8,128)S(1)} %scatter_custom_fusion.5), channel_id=1, source_target_pairs={{0,1},{1,2},{2,3},{3,4},{4,5},{5,6},{6,7},{7,0},{8,9},{9,10},{10,1... | collective-permute-start | bytes 259592 | tf_op jit(solution)/shard_map/ppermute | solution.py:18
  121.1 8.8 %all-to-all-start = ((f32[8,1,96]{2,1,0:T(1,128)}), f32[8,1,96]{2,1,0:T(1,128)S(1)}, u32[]{:S(2)}, u32[]{:S(2)}) async-start(f32[8,1,96]{2,1,0:T(1,128)} %bitcast.12), calls=%async_computation | async-start | bytes 8192 | tf_op jit(solution)/shard_map/all_to_all | solution.py:87
  131.1 1.3 collective-permute-start.8
  140.0 21.8 %copy-start.29 = (s32[1,81]{1,0:T(1,128)S(1)}, s32[1,81]{1,0:T(1,128)}, u32[]{:S(2)}) copy-start(s32[1,81]{1,0:T(1,128)} %param.41) | copy-start | bytes 976
  154.2 4.8 %collective-permute-start.9 = (f32[81]{0:T(128)S(1)}, f32[81]{0:T(128)S(1)}, u32[]{:S(2)}, u32[]{:S(2)}) collective-permute-start(f32[81]{0:T(128)S(1)} %scatter_custom_fusion.10), channel_id=1, source_target_pairs={{0,1},{1,2},{2,3},{3,4},{4,5},{5,6},{6,7},{7,0},{8,9},{9,10},{10,1... | collective-permute-start | bytes 980 | tf_op jit(solution)/shard_map/ppermute | solution.py:18
  159.0 1.6 collective-permute-start.10
  167.6 23.0 %copy-start.27 = (s32[8]{0:T(128)S(1)}, s32[8]{0:T(128)}, u32[]{:S(2)}) copy-start(s32[8]{0:T(128)} %fusion.60) | copy-start | bytes 100
  167.6 29.2 %copy-start.19 = (s32[1024]{0:T(1024)S(1)}, s32[1024]{0:T(1024)}, u32[]{:S(2)}) copy-start(s32[1024]{0:T(1024)} %copy-done.18) | copy-start | bytes 12292
  167.6 29.9 %copy-start.24 = (pred[169]{0:T(512)(128)(4,1)S(1)}, pred[169]{0:T(512)(128)(4,1)}, u32[]{:S(2)}) copy-start(pred[169]{0:T(512)(128)(4,1)} %copy-done.23) | copy-start | bytes 511
  181.7 4.8 %collective-permute-start.11 = (f32[81]{0:T(128)S(1)}, f32[81]{0:T(128)S(1)}, u32[]{:S(2)}, u32[]{:S(2)}) collective-permute-start(f32[81]{0:T(128)S(1)} %scatter_custom_fusion.12), channel_id=1, source_target_pairs={{0,1},{1,2},{2,3},{3,4},{4,5},{5,6},{6,7},{7,0},{8,9},{9,10},{10,1... | collective-permute-start | bytes 980 | tf_op jit(solution)/shard_map/ppermute | solution.py:18
  187.3 8.8 %all-to-all-start.1 = ((f32[8,1,96]{2,1,0:T(1,128)}), f32[8,1,96]{2,1,0:T(1,128)S(1)}, u32[]{:S(2)}, u32[]{:S(2)}) async-start(f32[8,1,96]{2,1,0:T(1,128)} %all_to_all.16), calls=%async_computation.1 | async-start | bytes 8192 | tf_op jit(solution)/shard_map/all_to_all | solution.py:87
  190.6 6.1 %collective-permute-start.6 = (bf16[169,128]{1,0:T(8,128)(2,1)S(1)}, bf16[169,128]{1,0:T(8,128)(2,1)S(1)}, u32[]{:S(2)}, u32[]{:S(2)}) collective-permute-start(bf16[169,128]{1,0:T(8,128)(2,1)S(1)} %slice.263), channel_id=1, source_target_pairs={{0,7},{1,0},{2,1},{3,2},{4,3},{5,4},{6,5},{7,6},{8,15},{9,8},{10,9... | collective-permute-start | bytes 129800 | tf_op jit(solution)/shard_map/ppermute | solution.py:18
  196.7 20.4 %copy-start.22 = (f32[768]{0:T(1024)}, f32[768]{0:T(1024)S(1)}, u32[]{:S(2)}) copy-start(f32[768]{0:T(1024)S(1)} %select_n.110) | copy-start | bytes 9220
  217.2 6.0 %collective-permute-start.7 = (f32[169,128]{1,0:T(8,128)}, f32[169,128]{1,0:T(8,128)S(1)}, u32[]{:S(2)}, u32[]{:S(2)}) collective-permute-start(f32[169,128]{1,0:T(8,128)} %scatter_custom_fusion.7), channel_id=1, source_target_pairs={{0,1},{1,2},{2,3},{3,4},{4,5},{5,6},{6,7},{7,0},{8,9},{9,10},{10,1... | collective-permute-start | bytes 259592 | tf_op jit(solution)/shard_map/ppermute | solution.py:18
  225.6 1.7 collective-permute-start.12
  235.4 24.0 %copy-start.16 = (f32[768]{0:T(1024)S(1)}, f32[768]{0:T(1024)}, u32[]{:S(2)}) copy-start(f32[768]{0:T(1024)} %copy-done.15) | copy-start | bytes 9220
  235.4 24.0 %copy-start.20 = (f32[768]{0:T(1024)S(1)}, f32[768]{0:T(1024)}, u32[]{:S(2)}) copy-start(f32[768]{0:T(1024)} %get-tuple-element.90) | copy-start | bytes 9220
  251.0 5.8 %collective-permute-start.13 = (f32[169,128]{1,0:T(8,128)S(1)}, f32[169,128]{1,0:T(8,128)S(1)}, u32[]{:S(2)}, u32[]{:S(2)}) collective-permute-start(f32[169,128]{1,0:T(8,128)S(1)} %scatter_custom_fusion.14), channel_id=1, source_target_pairs={{0,1},{1,2},{2,3},{3,4},{4,5},{5,6},{6,7},{7,0},{8,9},{9,10},{10,1... | collective-permute-start | bytes 259592 | tf_op jit(solution)/shard_map/ppermute | solution.py:18
  (16 other events, 143.1 us)
where the time goes:
time: 263 us; the launch traced here: 261 us
  other arithmetic  95.7 us (36%)
  local copies, waits for them, and re-layouts  82.8 us (31%)
  waiting for transfers between devices  40.4 us (15%)
  starting transfers between devices  17.3 us (7%)
  matrix products  13.9 us (5%)
  blocking collectives  9.88 us (4%)
    scatter-add x5, other arithmetic, cell_terms(): return jnp.zeros(local_rows.shape, jnp.float32).at[node_ids.reshape(-1)]....  48.8 us
    ppermute x14, waiting for transfers between devices, from_behind(): lax.ppermute(array, axis, [(i, (i + by) % length) for i in range(length)])  33 us
    gather x10, local copies, waits for them, and re-layouts, cell_terms(): cell_vals = jnp.take(local_rows, node_ids, axis=0)  26.1 us
    scatter-add x2, other arithmetic, field_terms(): jnp.zeros(local_rows.shape, jnp.float32).at[node_ids.reshape(-1)]  22.1 us
    gather x4, local copies, waits for them, and re-layouts, field_terms(): cell_vals = jnp.take(local_rows, node_ids, axis=0)  11.5 us
    ppermute x14, starting transfers between devices, from_behind(): lax.ppermute(array, axis, [(i, (i + by) % length) for i in range(length)])  10.7 us
    reshape x5, local copies, waits for them, and re-layouts, cell_terms(): product.reshape(-1, columns)  10.1 us
    psum x1, blocking collectives, band_total(): return lax.psum(values, 'band')  9.88 us
  transfers between devices with their start and end apart: 16, of which 14 were waited for; matrix products, arithmetic and copies ran while one was open for 7% of the time, Pallas kernels for 0%

commit v1 on v0

--- a/solution.py
+++ b/solution.py
@@ -88,7 +88,7 @@
 
 
 def band_total(values):
-    return lax.psum(values, "band")
+    return jnp.sum(lax.all_gather(values, "band"), axis=0)
 
 
 def per_device(

time: 263 us -> 262 us (level)
    psum x1 -> x0, blocking collectives: 9.88 us -> none  [band_total(): return lax.psum(values, 'band')]
    all_gather x0 -> x1, blocking collectives: none -> 8.2 us  [band_total(): return jnp.sum(lax.all_gather(values, 'band'), axis=0)]
where the time goes in v1:
time: 262 us; the launch traced here: 260 us
  other arithmetic  95.9 us (37%)
  local copies, waits for them, and re-layouts  82.8 us (32%)
  waiting for transfers between devices  40.2 us (15%)
  starting transfers between devices  17.3 us (7%)
  matrix products  13.9 us (5%)
  blocking collectives  8.2 us (3%)
    scatter-add x5, other arithmetic, cell_terms(): return jnp.zeros(local_rows.shape, jnp.float32).at[node_ids.reshape(-1)]....  48.9 us
    ppermute x14, waiting for transfers between devices, from_behind(): lax.ppermute(array, axis, [(i, (i + by) % length) for i in range(length)])  32.9 us
    gather x10, local copies, waits for them, and re-layouts, cell_terms(): cell_vals = jnp.take(local_rows, node_ids, axis=0)  26 us
    scatter-add x2, other arithmetic, field_terms(): jnp.zeros(local_rows.shape, jnp.float32).at[node_ids.reshape(-1)]  22.1 us
    gather x4, local copies, waits for them, and re-layouts, field_terms(): cell_vals = jnp.take(local_rows, node_ids, axis=0)  11.5 us
    ppermute x14, starting transfers between devices, from_behind(): lax.ppermute(array, axis, [(i, (i + by) % length) for i in range(length)])  10.7 us
    reshape x5, local copies, waits for them, and re-layouts, cell_terms(): product.reshape(-1, columns)  10.1 us
    dot_general x5, matrix products, cell_terms(): jnp.einsum('pq,cqm->cpm', cell_matrix, cell_vals, preferred_element_type=...  8.97 us
  transfers between devices with their start and end apart: 16, of which 14 were waited for; matrix products, arithmetic and copies ran while one was open for 7% of the time, Pallas kernels for 0%

profile of v1, /device:TPU:0, one launch (start us, length us, event | category | flops | bytes accessed | tf_op | source)
XLA Modules:
  0.0 259.7 jit_solution(16906665983128226566)
XLA Ops:
  1.8 4.6 %collective-permute-start = (bf16[169,128]{1,0:T(8,128)(2,1)S(1)}, bf16[169,128]{1,0:T(8,128)(2,1)S(1)}, u32[]{:S(2)}, u32[]{:S(2)}) collective-permute-start(bf16[169,128]{1,0:T(8,128)(2,1)S(1)} %slice.251), channel_id=1, source_target_pairs={{0,7},{1,0},{2,1},{3,2},{4,3},{5,4},{6,5},{7,6},{8,15},{9,8},{10,9... | collective-permute-start | bytes 129800 | tf_op jit(solution)/shard_map/ppermute | solution.py:18
  13.0 3.3 %gather_fusion.2 = bf16[1372,128]{1,0:T(8,128)(2,1)S(1)} fusion(bf16[937,128]{1,0:T(8,128)(2,1)S(1)} %pad_maximum_fusion, s32[2048]{0:T(1024)S(1)} %pad_clamp_fusion.1), kind=kCustom, calls=%fused_computation.1.clone | custom fusion | bytes 707952 | tf_op jit(solution)/shard_map/jit(_take)/gather | solution.py:62
  19.9 9.9 %scatter_custom_fusion = f32[937,128]{1,0:T(8,128)} fusion(s32[1372]{0:T(1024)S(1)} %fusion.51, f32[1372,128]{1,0:T(8,128)} %reshape.513, f32[]{:T(128)} %constant.234.clone.1), kind=kCustom, calls=%fused_computation.72 | custom fusion | flops 175616 | bytes 480256 | tf_op jit(solution)/shard_map/scatter-add | solution.py:68
  32.8 4.1 %collective-permute-done.1 = f32[169,128]{1,0:T(8,128)S(1)} collective-permute-done((f32[169,128]{1,0:T(8,128)S(1)}, f32[169,128]{1,0:T(8,128)S(1)}, u32[]{:S(2)}, u32[]{:S(2)}) %collective-permute-start.1) | collective-permute-done | bytes 86560 | tf_op jit(solution)/shard_map/ppermute | solution.py:18
  43.7 4.4 %gather_fusion.4 = bf16[1372,128]{1,0:T(8,128)(2,1)} fusion(bf16[937,128]{1,0:T(8,128)(2,1)S(1)} %pad_maximum_fusion.1, s32[2048]{0:T(1024)} %copy-done.7), kind=kCustom, calls=%fused_computation.8.clone | custom fusion | bytes 707952 | tf_op jit(solution)/shard_map/jit(_take)/gather | solution.py:62
  49.9 2.4 convolution_bitcast_fusion.3
  52.4 2.1 reshape.529
  54.4 9.9 %scatter_custom_fusion.2 = f32[937,128]{1,0:T(8,128)} fusion(s32[1372]{0:T(1024)} %copy-done.25, f32[1372,128]{1,0:T(8,128)} %reshape.529, f32[]{:T(128)} %constant.234.clone.1), kind=kCustom, calls=%fused_computation.70 | custom fusion | flops 175616 | bytes 480256 | tf_op jit(solution)/shard_map/scatter-add | solution.py:68
  68.1 3.4 %collective-permute-done.3 = f32[169,128]{1,0:T(8,128)S(1)} collective-permute-done((f32[169,128]{1,0:T(8,128)S(1)}, f32[169,128]{1,0:T(8,128)S(1)}, u32[]{:S(2)}, u32[]{:S(2)}) %collective-permute-start.3) | collective-permute-done | bytes 86560 | tf_op jit(solution)/shard_map/ppermute | solution.py:18
  79.1 4.0 %gather_fusion.6 = bf16[1372,128]{1,0:T(8,128)(2,1)} fusion(bf16[937,128]{1,0:T(8,128)(2,1)S(1)} %pad_maximum_fusion.2, s32[2048]{0:T(1024)S(1)} %copy-done.8), kind=kCustom, calls=%fused_computation.9.clone | custom fusion | bytes 707952 | tf_op jit(solution)/shard_map/jit(_take)/gather | solution.py:62
  87.6 9.9 %scatter_custom_fusion.4 = f32[937,128]{1,0:T(8,128)} fusion(s32[1372]{0:T(1024)} %copy-done.25, f32[1372,128]{1,0:T(8,128)} %reshape.545, f32[]{:T(128)} %constant.234.clone.1), kind=kCustom, calls=%fused_computation.68 | custom fusion | flops 175616 | bytes 480256 | tf_op jit(solution)/shard_map/scatter-add | solution.py:68
  100.7 4.0 %collective-permute-done.5 = f32[169,128]{1,0:T(8,128)S(1)} collective-permute-done((f32[169,128]{1,0:T(8,128)S(1)}, f32[169,128]{1,0:T(8,128)S(1)}, u32[]{:S(2)}, u32[]{:S(2)}) %collective-permute-start.5) | collective-permute-done | bytes 86560 | tf_op jit(solution)/shard_map/ppermute | solution.py:18
  109.8 8.2 %all-gather.1 = f32[4,1,768]{2,1,0:T(1,128)S(1)} all-gather(f32[1,1,768]{2,1,0:T(1,128)S(1)} %convolution_bitcast_fusion.5), channel_id=2, replica_groups=mesh['band'=4,'domain'=8] {'band'}, dimensions={0}, use_global_device_ids=true | all-gather | bytes 15360 | tf_op jit(solution)/shard_map/all_gather | solution.py:91
  119.4 3.3 %all-to-all-start = ((f32[8,1,96]{2,1,0:T(1,128)}), f32[8,1,96]{2,1,0:T(1,128)S(1)}, u32[]{:S(2)}, u32[]{:S(2)}) async-start(f32[8,1,96]{2,1,0:T(1,128)} %bitcast.12), calls=%async_computation | async-start | bytes 8192 | tf_op jit(solution)/shard_map/all_to_all | solution.py:87
  122.7 5.4 %all-to-all-done = f32[8,1,96]{2,1,0:T(1,128)S(1)} async-done(((f32[8,1,96]{2,1,0:T(1,128)}), f32[8,1,96]{2,1,0:T(1,128)S(1)}, u32[]{:S(2)}, u32[]{:S(2)}) %all-to-all-start) | async-done | bytes 3104 | tf_op jit(solution)/shard_map/all_to_all | solution.py:87
  132.7 5.6 %gather_fusion.10 = f32[1458]{0:T(1024)S(1)} fusion(f32[849]{0:T(1024)S(1)} %pad_maximum_fusion.5, s32[2048]{0:T(1024)S(1)} %pad_clamp_fusion), kind=kCustom, calls=%fused_computation.3.clone | custom fusion | bytes 17496 | tf_op jit(solution)/shard_map/jit(_take)/gather | solution.py:73
  140.5 11.0 %scatter_custom_fusion.9 = f32[849]{0:T(1024)S(1)} fusion(s32[1458]{0:T(1024)S(1)} %fusion.46, f32[1458]{0:T(1024)S(1)} %reshape.585, f32[]{:T(128)} %constant.234.clone.1), kind=kCustom, calls=%fused_computation.137 | custom fusion | flops 1458 | bytes 3400 | tf_op jit(solution)/shard_map/scatter-add | solution.py:82
  154.0 3.3 %collective-permute-done.9 = f32[81]{0:T(128)S(1)} collective-permute-done((f32[81]{0:T(128)S(1)}, f32[81]{0:T(128)S(1)}, u32[]{:S(2)}, u32[]{:S(2)}) %collective-permute-start.9) | collective-permute-done | bytes 356 | tf_op jit(solution)/shard_map/ppermute | solution.py:18
  160.2 5.7 %gather_fusion.12 = f32[1458]{0:T(1024)S(1)} fusion(f32[849]{0:T(1024)S(1)} %pad_maximum_fusion.6, s32[2048]{0:T(1024)S(1)} %pad_clamp_fusion), kind=kCustom, calls=%fused_computation.13.clone | custom fusion | bytes 17496 | tf_op jit(solution)/shard_map/jit(_take)/gather | solution.py:73
  168.0 11.0 %scatter_custom_fusion.11 = f32[849]{0:T(1024)S(1)} fusion(s32[1458]{0:T(1024)S(1)} %fusion.46, f32[1458]{0:T(1024)S(1)} %reshape.601, f32[]{:T(128)} %constant.234.clone.1), kind=kCustom, calls=%fused_computation.135 | custom fusion | flops 1458 | bytes 3400 | tf_op jit(solution)/shard_map/scatter-add | solution.py:82
  180.1 4.7 %collective-permute-done.11 = f32[81]{0:T(128)S(1)} collective-permute-done((f32[81]{0:T(128)S(1)}, f32[81]{0:T(128)S(1)}, u32[]{:S(2)}, u32[]{:S(2)}) %collective-permute-start.11) | collective-permute-done | bytes 356 | tf_op jit(solution)/shard_map/ppermute | solution.py:18
  185.6 3.3 %all-to-all-start.1 = ((f32[8,1,96]{2,1,0:T(1,128)}), f32[8,1,96]{2,1,0:T(1,128)S(1)}, u32[]{:S(2)}, u32[]{:S(2)}) async-start(f32[8,1,96]{2,1,0:T(1,128)} %all_to_all.16), calls=%async_computation.1 | async-start | bytes 8192 | tf_op jit(solution)/shard_map/all_to_all | solution.py:87
  188.9 3.5 %collective-permute-start.6 = (bf16[169,128]{1,0:T(8,128)(2,1)S(1)}, bf16[169,128]{1,0:T(8,128)(2,1)S(1)}, u32[]{:S(2)}, u32[]{:S(2)}) collective-permute-start(bf16[169,128]{1,0:T(8,128)(2,1)S(1)} %slice.263), channel_id=1, source_target_pairs={{0,7},{1,0},{2,1},{3,2},{4,3},{5,4},{6,5},{7,6},{8,15},{9,8},{10,9... | collective-permute-start | bytes 129800 | tf_op jit(solution)/shard_map/ppermute | solution.py:18
  195.9 4.0 %gather_fusion.8 = bf16[1372,128]{1,0:T(8,128)(2,1)} fusion(bf16[937,128]{1,0:T(8,128)(2,1)S(1)} %pad_maximum_fusion.3, s32[2048]{0:T(1024)S(1)} %copy-done.8), kind=kCustom, calls=%fused_computation.10.clone | custom fusion | bytes 707952 | tf_op jit(solution)/shard_map/jit(_take)/gather | solution.py:62
  204.5 9.3 %scatter_custom_fusion.6 = f32[937,128]{1,0:T(8,128)S(1)} fusion(s32[1372]{0:T(1024)} %copy-done.25, f32[1372,128]{1,0:T(8,128)} %reshape.561, f32[]{:T(128)} %constant.234.clone.1), kind=kCustom, calls=%fused_computation.66 | custom fusion | flops 175616 | bytes 480256 | tf_op jit(solution)/shard_map/scatter-add | solution.py:68
  217.1 4.3 %collective-permute-done.7 = f32[169,128]{1,0:T(8,128)S(1)} collective-permute-done((f32[169,128]{1,0:T(8,128)}, f32[169,128]{1,0:T(8,128)S(1)}, u32[]{:S(2)}, u32[]{:S(2)}) %collective-permute-start.7) | collective-permute-done | bytes 86560 | tf_op jit(solution)/shard_map/ppermute | solution.py:18
  227.5 4.4 %gather_fusion.14 = bf16[1372,128]{1,0:T(8,128)(2,1)} fusion(bf16[937,128]{1,0:T(8,128)(2,1)S(1)} %pad_maximum_fusion.4, s32[2048]{0:T(1024)} %copy-done.7), kind=kCustom, calls=%fused_computation.11.clone | custom fusion | bytes 707952 | tf_op jit(solution)/shard_map/jit(_take)/gather | solution.py:62
  233.7 2.4 convolution_bitcast_fusion
  236.0 2.0 reshape.617
  238.0 9.9 %scatter_custom_fusion.13 = f32[937,128]{1,0:T(8,128)} fusion(s32[1372]{0:T(1024)} %copy-done.25, f32[1372,128]{1,0:T(8,128)} %reshape.617, f32[]{:T(128)} %constant.234.clone.1), kind=kCustom, calls=%fused_computation.64 | custom fusion | flops 175616 | bytes 480256 | tf_op jit(solution)/shard_map/scatter-add | solution.py:68
  251.1 4.0 %collective-permute-done.13 = f32[169,128]{1,0:T(8,128)S(1)} collective-permute-done((f32[169,128]{1,0:T(8,128)S(1)}, f32[169,128]{1,0:T(8,128)S(1)}, u32[]{:S(2)}, u32[]{:S(2)}) %collective-permute-start.13) | collective-permute-done | bytes 86560 | tf_op jit(solution)/shard_map/ppermute | solution.py:18
  257.6 2.0 multiply_subtract_fusion
  (199 shorter events, 88.9 us)
Async XLA Ops:
  0.6 137.8 %copy-start = (f32[729,729]{1,0:T(8,128)S(1)}, f32[729,729]{1,0:T(8,128)}, u32[]{:S(2)}) copy-start(f32[729,729]{1,0:T(8,128)} %param.39) | copy-start | bytes 6377296
  1.8 10.3 %collective-permute-start = (bf16[169,128]{1,0:T(8,128)(2,1)S(1)}, bf16[169,128]{1,0:T(8,128)(2,1)S(1)}, u32[]{:S(2)}, u32[]{:S(2)}) collective-permute-start(bf16[169,128]{1,0:T(8,128)(2,1)S(1)} %slice.251), channel_id=1, source_target_pairs={{0,7},{1,0},{2,1},{3,2},{4,3},{5,4},{6,5},{7,6},{8,15},{9,8},{10,9... | collective-permute-start | bytes 129800 | tf_op jit(solution)/shard_map/ppermute | solution.py:18
  16.5 22.1 %copy-start.2 = (f32[768,128]{1,0:T(8,128)S(1)}, f32[768,128]{1,0:T(8,128)}, u32[]{:S(2)}) copy-start(f32[768,128]{1,0:T(8,128)} %param.33) | copy-start | bytes 1179652
  31.2 5.8 %collective-permute-start.1 = (f32[169,128]{1,0:T(8,128)S(1)}, f32[169,128]{1,0:T(8,128)S(1)}, u32[]{:S(2)}, u32[]{:S(2)}) collective-permute-start(f32[169,128]{1,0:T(8,128)S(1)} %scatter_custom_fusion.1), channel_id=1, source_target_pairs={{0,1},{1,2},{2,3},{3,4},{4,5},{5,6},{6,7},{7,0},{8,9},{9,10},{10,1... | collective-permute-start | bytes 259592 | tf_op jit(solution)/shard_map/ppermute | solution.py:18
  39.5 1.8 collective-permute-start.2
  49.9 24.1 %copy-start.4 = (f32[768,128]{1,0:T(8,128)S(1)}, f32[768,128]{1,0:T(8,128)}, u32[]{:S(2)}) copy-start(f32[768,128]{1,0:T(8,128)} %copy-done.3) | copy-start | bytes 1179652
  49.9 24.1 %copy-start.10 = (f32[768]{0:T(1024)S(1)}, f32[768]{0:T(1024)}, u32[]{:S(2)}) copy-start(f32[768]{0:T(1024)} %param.34) | copy-start | bytes 9220
  49.9 24.1 %copy-start.14 = (f32[768]{0:T(1024)S(1)}, f32[768]{0:T(1024)}, u32[]{:S(2)}) copy-start(f32[768]{0:T(1024)} %broadcast_multiply_fusion.2) | copy-start | bytes 9220
  52.4 23.3 %copy-start.30 = (s32[1,8]{1,0:T(1,128)S(1)}, s32[1,8]{1,0:T(1,128)}, u32[]{:S(2)}) copy-start(s32[1,8]{1,0:T(1,128)} %param.43) | copy-start | bytes 100
  52.4 23.9 %copy-start.11 = (s32[2,729]{1,0:T(2,128)S(1)}, s32[2,729]{1,0:T(2,128)}, u32[]{:S(2)}) copy-start(s32[2,729]{1,0:T(2,128)} %param.40) | copy-start | bytes 17500
  52.4 24.0 %copy-start.17 = (s32[2,729]{1,0:T(2,128)S(1)}, s32[2,729]{1,0:T(2,128)}, u32[]{:S(2)}) copy-start(s32[2,729]{1,0:T(2,128)} %compare_select_fusion.2) | copy-start | bytes 17500
  54.4 24.6 %copy-start.8 = (s32[2048]{0:T(1024)S(1)}, s32[2048]{0:T(1024)}, u32[]{:S(2)}) copy-start(s32[2048]{0:T(1024)} %copy-done.7) | copy-start | bytes 24580
  65.7 5.8 %collective-permute-start.3 = (f32[169,128]{1,0:T(8,128)S(1)}, f32[169,128]{1,0:T(8,128)S(1)}, u32[]{:S(2)}, u32[]{:S(2)}) collective-permute-start(f32[169,128]{1,0:T(8,128)S(1)} %scatter_custom_fusion.3), channel_id=1, source_target_pairs={{0,1},{1,2},{2,3},{3,4},{4,5},{5,6},{6,7},{7,0},{8,9},{9,10},{10,1... | collective-permute-start | bytes 259592 | tf_op jit(solution)/shard_map/ppermute | solution.py:18
  75.3 2.1 collective-permute-start.4
  98.8 5.8 %collective-permute-start.5 = (f32[169,128]{1,0:T(8,128)S(1)}, f32[169,128]{1,0:T(8,128)S(1)}, u32[]{:S(2)}, u32[]{:S(2)}) collective-permute-start(f32[169,128]{1,0:T(8,128)S(1)} %scatter_custom_fusion.5), channel_id=1, source_target_pairs={{0,1},{1,2},{2,3},{3,4},{4,5},{5,6},{6,7},{7,0},{8,9},{9,10},{10,1... | collective-permute-start | bytes 259592 | tf_op jit(solution)/shard_map/ppermute | solution.py:18
  119.4 8.8 %all-to-all-start = ((f32[8,1,96]{2,1,0:T(1,128)}), f32[8,1,96]{2,1,0:T(1,128)S(1)}, u32[]{:S(2)}, u32[]{:S(2)}) async-start(f32[8,1,96]{2,1,0:T(1,128)} %bitcast.12), calls=%async_computation | async-start | bytes 8192 | tf_op jit(solution)/shard_map/all_to_all | solution.py:87
  129.4 1.3 collective-permute-start.8
  138.3 21.8 %copy-start.29 = (s32[1,81]{1,0:T(1,128)S(1)}, s32[1,81]{1,0:T(1,128)}, u32[]{:S(2)}) copy-start(s32[1,81]{1,0:T(1,128)} %param.41) | copy-start | bytes 976
  152.5 4.8 %collective-permute-start.9 = (f32[81]{0:T(128)S(1)}, f32[81]{0:T(128)S(1)}, u32[]{:S(2)}, u32[]{:S(2)}) collective-permute-start(f32[81]{0:T(128)S(1)} %scatter_custom_fusion.10), channel_id=1, source_target_pairs={{0,1},{1,2},{2,3},{3,4},{4,5},{5,6},{6,7},{7,0},{8,9},{9,10},{10,1... | collective-permute-start | bytes 980 | tf_op jit(solution)/shard_map/ppermute | solution.py:18
  157.3 1.6 collective-permute-start.10
  165.9 23.0 %copy-start.27 = (s32[8]{0:T(128)S(1)}, s32[8]{0:T(128)}, u32[]{:S(2)}) copy-start(s32[8]{0:T(128)} %fusion.60) | copy-start | bytes 100
  165.9 29.2 %copy-start.19 = (s32[1024]{0:T(1024)S(1)}, s32[1024]{0:T(1024)}, u32[]{:S(2)}) copy-start(s32[1024]{0:T(1024)} %copy-done.18) | copy-start | bytes 12292
  165.9 29.9 %copy-start.24 = (pred[169]{0:T(512)(128)(4,1)S(1)}, pred[169]{0:T(512)(128)(4,1)}, u32[]{:S(2)}) copy-start(pred[169]{0:T(512)(128)(4,1)} %copy-done.23) | copy-start | bytes 511
  180.0 4.8 %collective-permute-start.11 = (f32[81]{0:T(128)S(1)}, f32[81]{0:T(128)S(1)}, u32[]{:S(2)}, u32[]{:S(2)}) collective-permute-start(f32[81]{0:T(128)S(1)} %scatter_custom_fusion.12), channel_id=1, source_target_pairs={{0,1},{1,2},{2,3},{3,4},{4,5},{5,6},{6,7},{7,0},{8,9},{9,10},{10,1... | collective-permute-start | bytes 980 | tf_op jit(solution)/shard_map/ppermute | solution.py:18
  185.6 8.8 %all-to-all-start.1 = ((f32[8,1,96]{2,1,0:T(1,128)}), f32[8,1,96]{2,1,0:T(1,128)S(1)}, u32[]{:S(2)}, u32[]{:S(2)}) async-start(f32[8,1,96]{2,1,0:T(1,128)} %all_to_all.16), calls=%async_computation.1 | async-start | bytes 8192 | tf_op jit(solution)/shard_map/all_to_all | solution.py:87
  188.9 6.1 %collective-permute-start.6 = (bf16[169,128]{1,0:T(8,128)(2,1)S(1)}, bf16[169,128]{1,0:T(8,128)(2,1)S(1)}, u32[]{:S(2)}, u32[]{:S(2)}) collective-permute-start(bf16[169,128]{1,0:T(8,128)(2,1)S(1)} %slice.263), channel_id=1, source_target_pairs={{0,7},{1,0},{2,1},{3,2},{4,3},{5,4},{6,5},{7,6},{8,15},{9,8},{10,9... | collective-permute-start | bytes 129800 | tf_op jit(solution)/shard_map/ppermute | solution.py:18
  195.0 20.4 %copy-start.22 = (f32[768]{0:T(1024)}, f32[768]{0:T(1024)S(1)}, u32[]{:S(2)}) copy-start(f32[768]{0:T(1024)S(1)} %select_n.110) | copy-start | bytes 9220
  215.5 6.0 %collective-permute-start.7 = (f32[169,128]{1,0:T(8,128)}, f32[169,128]{1,0:T(8,128)S(1)}, u32[]{:S(2)}, u32[]{:S(2)}) collective-permute-start(f32[169,128]{1,0:T(8,128)} %scatter_custom_fusion.7), channel_id=1, source_target_pairs={{0,1},{1,2},{2,3},{3,4},{4,5},{5,6},{6,7},{7,0},{8,9},{9,10},{10,1... | collective-permute-start | bytes 259592 | tf_op jit(solution)/shard_map/ppermute | solution.py:18
  223.9 1.7 collective-permute-start.12
  233.7 24.0 %copy-start.16 = (f32[768]{0:T(1024)S(1)}, f32[768]{0:T(1024)}, u32[]{:S(2)}) copy-start(f32[768]{0:T(1024)} %copy-done.15) | copy-start | bytes 9220
  233.7 24.0 %copy-start.20 = (f32[768]{0:T(1024)S(1)}, f32[768]{0:T(1024)}, u32[]{:S(2)}) copy-start(f32[768]{0:T(1024)} %get-tuple-element.90) | copy-start | bytes 9220
  249.3 5.8 %collective-permute-start.13 = (f32[169,128]{1,0:T(8,128)S(1)}, f32[169,128]{1,0:T(8,128)S(1)}, u32[]{:S(2)}, u32[]{:S(2)}) collective-permute-start(f32[169,128]{1,0:T(8,128)S(1)} %scatter_custom_fusion.14), channel_id=1, source_target_pairs={{0,1},{1,2},{2,3},{3,4},{4,5},{5,6},{6,7},{7,0},{8,9},{9,10},{10,1... | collective-permute-start | bytes 259592 | tf_op jit(solution)/shard_map/ppermute | solution.py:18
  (16 other events, 143.2 us)
